TPU v7x, 512 devices: a whole 4x8x8 slice. The times are simulated.
512 devices in a mesh: dp: 128 (over y, z, core), rep: 4 (over x).
Axes of the slice: x: 4, y: 8, z: 8, core: 2. Of those that a mesh axis runs over, the one named last changes fastest.
Arguments:
- gradient_receptance: bfloat16 [128, 4, 2, 768, 768], P('dp', 'rep'), may hold values from -1000 to 1000
- gradient_factors: bfloat16 [128, 4, 2, 768, 256], P('dp', 'rep'), may hold values from -1000 to 1000
- gradient_channels: bfloat16 [128, 4, 2, 768, 16], P('dp', 'rep'), may hold values from -1000 to 1000
- primary_receptance: float32 [768, 768], P('dp'), may hold values from -0.21875 to 0.21875
- primary_factors: float32 [768, 256], P('dp'), may hold values from -0.21875 to 0.21875
- primary_channels: float32 [768, 16], P('dp'), may hold values from -1 to 1
- first_moment_receptance: float32 [768, 768], P('dp'), may hold values from -0.00390625 to 0.00390625
- first_moment_factors: float32 [768, 256], P('dp'), may hold values from -0.00390625 to 0.00390625
- first_moment_channels: float32 [768, 16], P('dp'), may hold values from -0.00390625 to 0.00390625
- second_moment_receptance: float32 [768, 768], P('dp'), may hold values from 1e-08 to 1e-06
- second_moment_factors: float32 [768, 256], P('dp'), may hold values from 1e-08 to 1e-06
- second_moment_channels: float32 [768, 16], P('dp'), may hold values from 1e-08 to 1e-06
Outputs:
- weight_receptance: bfloat16 [768, 768], replicated
- weight_lora: bfloat16 [768, 256], replicated
- weight_vectors: bfloat16 [768, 16], replicated
- new_master_receptance: float32 [768, 768], P('dp')
- new_master_lora: float32 [768, 256], P('dp')
- new_master_vectors: float32 [768, 16], P('dp')
- new_first_receptance: float32 [768, 768], P('dp')
- new_first_lora: float32 [768, 256], P('dp')
- new_first_vectors: float32 [768, 16], P('dp')
- new_second_receptance: float32 [768, 768], P('dp')
- new_second_lora: float32 [768, 256], P('dp')
- new_second_vectors: float32 [768, 16], P('dp')
All inputs are finite; a program needn't handle non-finite values.
Results may differ from a plain program's by a relative error of at most 0.001.
Values may be sent and summed in bfloat16 or wider, within the bound.
A program may use at most 64 MiB of HBM per device.

v0:
```python
import jax
import jax.numpy as jnp
from jax import lax
from jax.sharding import PartitionSpec as P

STEP = 20


beta_one = 0.9
beta_two = 0.99
adam_eps = 1e-08
learn_rate = 0.001
weight_decay_rate = 0.1
max_norm = 1.0
norm_eps = 1e-06


def decoupled_adam_step(gradient, master, first, second, decay):
    new_first = beta_one * first + (1.0 - beta_one) * gradient
    new_second = beta_two * second + (1.0 - beta_two) * gradient * gradient
    update = (
        new_first
        / (1.0 - beta_one**STEP)
        / (jnp.sqrt(new_second / (1.0 - beta_two**STEP)) + adam_eps)
    )
    new_master = master - learn_rate * (update + decay * master)
    return (new_master, new_first, new_second)


def body(
    gradient_receptance,
    gradient_factors,
    gradient_channels,
    primary_receptance,
    primary_factors,
    primary_channels,
    first_moment_receptance,
    first_moment_factors,
    first_moment_channels,
    second_moment_receptance,
    second_moment_factors,
    second_moment_channels,
):
    row_count = primary_receptance.shape[0]
    receptance_width = primary_receptance.shape[1]
    factor_width = primary_factors.shape[1]
    local_sum = jnp.concatenate(
        [
            jnp.sum(gradient_receptance, axis=(0, 1, 2), dtype=jnp.float32),
            jnp.sum(gradient_factors, axis=(0, 1, 2), dtype=jnp.float32),
            jnp.sum(gradient_channels, axis=(0, 1, 2), dtype=jnp.float32),
        ],
        axis=1,
    )
    full_sum = lax.psum(local_sum, ("dp", "rep"))
    square_sum = jnp.sum(full_sum * full_sum)
    owned_rows = lax.dynamic_slice_in_dim(full_sum, lax.axis_index("dp") * row_count, row_count, 0)
    clipping_ratio = jnp.minimum(1.0, max_norm / (jnp.sqrt(square_sum) + norm_eps))
    gradient_clipped = clipping_ratio * owned_rows
    separate_factors = receptance_width + factor_width
    receptance_part = decoupled_adam_step(
        gradient_clipped[:, :receptance_width],
        primary_receptance,
        first_moment_receptance,
        second_moment_receptance,
        weight_decay_rate,
    )
    lowrank_factors = decoupled_adam_step(
        gradient_clipped[:, receptance_width:separate_factors],
        primary_factors,
        first_moment_factors,
        second_moment_factors,
        weight_decay_rate,
    )
    channel_vectors = decoupled_adam_step(
        gradient_clipped[:, separate_factors:],
        primary_channels,
        first_moment_channels,
        second_moment_channels,
        0.0,
    )
    packed_gradients = jnp.concatenate(
        [receptance_part[0], lowrank_factors[0], channel_vectors[0]], axis=1
    ).astype(jnp.bfloat16)
    collected_parts = lax.all_gather(packed_gradients, "dp", axis=0, tiled=True)
    return (
        collected_parts[:, :receptance_width],
        collected_parts[:, receptance_width:separate_factors],
        collected_parts[:, separate_factors:],
        receptance_part[0],
        lowrank_factors[0],
        channel_vectors[0],
        receptance_part[1],
        lowrank_factors[1],
        channel_vectors[1],
        receptance_part[2],
        lowrank_factors[2],
        channel_vectors[2],
    )


def solution(mesh):
    placed = (
        P("dp", "rep", None, None, None),
        P("dp", "rep", None, None, None),
        P("dp", "rep", None, None, None),
        P("dp", None),
        P("dp", None),
        P("dp", None),
        P("dp", None),
        P("dp", None),
        P("dp", None),
        P("dp", None),
        P("dp", None),
        P("dp", None),
    )
    return jax.shard_map(
        body,
        mesh=mesh,
        in_specs=placed,
        out_specs=(
            P(),
            P(),
            P(),
            P("dp", None),
            P("dp", None),
            P("dp", None),
            P("dp", None),
            P("dp", None),
            P("dp", None),
            P("dp", None),
            P("dp", None),
            P("dp", None),
        ),
        check_vma=False,
    )
```

profile of v0, /device:TPU:1, one launch (start us, length us, event | category | flops | bytes accessed | tf_op | source)
XLA Modules:
  0.0 402.7 jit_solution(3003062648250207814)
XLA Ops:
  7.2 0.0 all-reduce.2.cloned.1.call-start
  7.2 0.8 convert_reduce_fusion.2
  8.0 0.2 copy.26
  8.2 1.3 convert_reduce_fusion.1
  9.5 2.3 convert_reduce_fusion
  11.9 2.0 pad_maximum_fusion
  13.9 0.0 copy-start.6
  13.9 0.0 copy-start.7
  13.9 0.0 copy-start.8
  13.9 0.0 copy-start.3
  13.9 0.0 copy-start.4
  13.9 0.0 copy-start.5
  13.9 0.0 copy-start
  13.9 0.0 copy-start.1
  14.0 0.0 copy-start.2
  14.0 0.0 all-reduce.2.cloned.1.call-update
  14.0 0.0 all-gather.3.cloned.1.call-start
  14.1 288.3 %all-reduce.2.cloned.1.call-done = f32[768,1040]{1,0:T(8,128)} async-done(((f32[768,1040]{1,0:T(8,128)}), f32[768,1040]{1,0:T(8,128)}) %all-reduce.2.cloned.1.call-update) | async-done | bytes 3194896 | tf_op jit(solution)/shard_map/psum | solution.py:55
  302.3 3.5 multiply_reduce_fusion
  306.6 0.9 dynamic-slice_multiply_fusion
  307.5 0.0 copy-done.6
  307.5 0.0 copy-done.7
  307.5 0.0 copy-done.8
  307.5 0.6 fusion.7
  308.1 0.0 copy-done.3
  308.1 0.0 copy-done.4
  308.1 0.0 copy-done.5
  308.2 0.6 fusion.5
  308.8 0.0 copy-done
  308.8 0.0 copy-done.1
  308.8 0.0 copy-done.2
  308.8 0.6 fusion.3
  309.4 0.6 maximum_bitcast_fusion
  310.0 0.0 all-gather.3.cloned.1.call-update
  310.1 80.3 %all-gather.3.cloned.1.call-done = bf16[128,6,1040]{2,1,0:T(8,128)(2,1)} async-done(((bf16[1,6,1040]{2,1,0:T(8,128)(2,1)}), bf16[128,6,1040]{2,1,0:T(8,128)(2,1)}) %all-gather.3.cloned.1.call-update) | async-done | bytes 1597456 | tf_op jit(solution)/shard_map/all_gather | solution.py:85
  390.3 3.0 reshape.25
  393.3 1.1 slice.27
  394.4 0.8 slice.28
  395.2 0.7 copy.27
  (1 shorter events, 0.0 us)
Async XLA Ops:
  7.2 295.2 %all-reduce.2.cloned.1.call-start = ((), (), s32[]{:S(2)}) async-start(), calls=%async_computation | async-start | bytes 7077888 | tf_op jit(solution)/shard_map/psum | solution.py:55
  13.9 293.6 %copy-start.6 = (f32[6,16]{1,0:T(8,128)S(1)}, f32[6,16]{1,0:T(8,128)}, u32[]{:S(2)}) copy-start(f32[6,16]{1,0:T(8,128)} %param.17) | copy-start | bytes 1156
  13.9 293.6 %copy-start.7 = (f32[6,16]{1,0:T(8,128)S(1)}, f32[6,16]{1,0:T(8,128)}, u32[]{:S(2)}) copy-start(f32[6,16]{1,0:T(8,128)} %param.20) | copy-start | bytes 1156
  13.9 293.6 %copy-start.8 = (f32[6,16]{1,0:T(8,128)S(1)}, f32[6,16]{1,0:T(8,128)}, u32[]{:S(2)}) copy-start(f32[6,16]{1,0:T(8,128)} %param.23) | copy-start | bytes 1156
  13.9 294.2 %copy-start.3 = (f32[6,256]{1,0:T(8,128)S(1)}, f32[6,256]{1,0:T(8,128)}, u32[]{:S(2)}) copy-start(f32[6,256]{1,0:T(8,128)} %param.16) | copy-start | bytes 18436
  13.9 294.2 %copy-start.4 = (f32[6,256]{1,0:T(8,128)S(1)}, f32[6,256]{1,0:T(8,128)}, u32[]{:S(2)}) copy-start(f32[6,256]{1,0:T(8,128)} %param.19) | copy-start | bytes 18436
  13.9 294.2 %copy-start.5 = (f32[6,256]{1,0:T(8,128)S(1)}, f32[6,256]{1,0:T(8,128)}, u32[]{:S(2)}) copy-start(f32[6,256]{1,0:T(8,128)} %param.22) | copy-start | bytes 18436
  13.9 294.8 %copy-start = (f32[6,768]{1,0:T(8,128)S(1)}, f32[6,768]{1,0:T(8,128)}, u32[]{:S(2)}) copy-start(f32[6,768]{1,0:T(8,128)} %param.15) | copy-start | bytes 55300
  13.9 294.8 %copy-start.1 = (f32[6,768]{1,0:T(8,128)S(1)}, f32[6,768]{1,0:T(8,128)}, u32[]{:S(2)}) copy-start(f32[6,768]{1,0:T(8,128)} %param.18) | copy-start | bytes 55300
  14.0 294.8 %copy-start.2 = (f32[6,768]{1,0:T(8,128)S(1)}, f32[6,768]{1,0:T(8,128)}, u32[]{:S(2)}) copy-start(f32[6,768]{1,0:T(8,128)} %param.21) | copy-start | bytes 55300
  14.0 376.3 %all-gather.3.cloned.1.call-start = ((), (), s32[]{:S(2)}) async-start(), calls=%async_computation.1 | async-start | bytes 2377728 | tf_op jit(solution)/shard_map/all_gather | solution.py:85
Sparse Core Ops, SparseCore 0:
  14.1 288.1 all-reduce.1
  310.2 80.0 all-gather.2
where the time goes:
time: 403 us
  waiting for transfers between devices  369 us (92%)
  between operations  14.9 us (4%)
  other arithmetic  13.4 us (3%)
  local copies, waits for them, and re-layouts  5.78 us (1%)
    psum x1, waiting for transfers between devices, body(): full_sum = lax.psum(local_sum, ('dp', 'rep'))  288 us
    all_gather x1, waiting for transfers between devices, body(): collected_parts = lax.all_gather(packed_gradients, 'dp', axis=0, tiled=True)  80.3 us
  transfers between devices with their start and end apart: 2, of which 2 were waited for; matrix products, arithmetic and copies ran while one was open for 0% of the time, Pallas kernels for 0%

commit v1 on v0

v1 whole, which is shorter than its diff:
```python
import functools

import jax
import jax.numpy as jnp
from jax import lax
from jax.experimental import pallas as pl
from jax.experimental.pallas import tpu as pltpu
from jax.sharding import PartitionSpec as P

STEP = 20
NZ = 8

beta_one = 0.9
beta_two = 0.99
adam_eps = 1e-08
learn_rate = 0.001
weight_decay_rate = 0.1
max_norm = 1.0
norm_eps = 1e-06

MESH = pl.DeviceIdType.MESH
f32 = jnp.float32
bf16 = jnp.bfloat16

STREAMS = ((1, 0), (1, 1), (-1, 1), (-1, 0))
LONG = (True, False, True, False)


def adam(g, master, first, second, decay):
    new_first = beta_one * first + (1.0 - beta_one) * g
    new_second = beta_two * second + (1.0 - beta_two) * g * g
    update = (
        new_first
        / (1.0 - beta_one**STEP)
        / (jnp.sqrt(new_second / (1.0 - beta_two**STEP)) + adam_eps)
    )
    new_master = master - learn_rate * (update + decay * master)
    return new_master, new_first, new_second


def kernel(
    ny, nz, nx,
    rec, fac, chg, mrec, mfac, frec, ffac, srec, sfac, chs,
    wrec, wfac, wch, omrec, omfac, ofrec, offac, osrec, osfac, och,
    own, part, chp, acc, rbuf, zs, zr, xb, sb, sws, swr, n1, n2, hb, ar, bb, zag, asm, w,
    own_sem, pair_s, pair_r, chp_s, chp_r, rs_s, rs_r, z_s, z_r, x_s, x_r, sw_sem,
    n1_s, n1_r, n2_s, n2_r, ag_sem, zag_s, zag_r, yag_s, yag_r, pc_s, pc_r, po_s, po_r,
):
    cr = 12 * nz
    half = ny // 2
    dp = lax.axis_index("dp")
    x = lax.axis_index("rep")
    c = lax.rem(dp, 2)
    z = lax.rem(dp // 2, nz)
    y = dp // (2 * nz)
    d = 1 - c

    def at(yy, zz, cc, xx):
        return ((yy * nz + zz) * 2 + cc, xx)

    def yo(o):
        return lax.rem(y + o + ny, ny)

    def zo(o):
        return lax.rem(z + o, nz)

    def xo(o):
        return lax.rem(x + o, nx)

    def remote(src, dst, ss, rs, dev):
        return pltpu.make_async_remote_copy(
            src_ref=src, dst_ref=dst, send_sem=ss, recv_sem=rs, device_id=dev, device_id_type=MESH
        )

    partner = at(y, z, d, x)

    own0 = pltpu.make_async_copy(
        rec.at[0, 0, :, :, pl.ds(pl.multiple_of(c * 512, 256), 256)], own.at[0], own_sem.at[0]
    )
    own0.start()

    @pl.when(c == 0)
    def _():
        pltpu.make_async_copy(rec.at[0, 0, :, :, pl.ds(256, 256)], own.at[1], own_sem.at[1]).start()

    @pl.when(c == 1)
    def _():
        pltpu.make_async_copy(fac.at[0, 0], own.at[1], own_sem.at[1]).start()

    barrier = pltpu.get_barrier_semaphore()
    peers = [partner]
    for o in range(1, nz):
        peers += [at(y, zo(o), c, x), at(y, zo(o), d, x)]
    for o in range(1, ny):
        peers.append(at(yo(o), z, c, x))
    for o in range(1, nx):
        peers.append(at(y, z, c, xo(o)))
    for dev in peers:
        pl.semaphore_signal(barrier, inc=1, device_id=dev, device_id_type=MESH)
    pl.semaphore_wait(barrier, len(peers))

    order = [half]
    for o in range(half - 1, 0, -1):
        order += [o, ny - o]
    order.append(0)

    def rows_of(k):
        return pl.ds(pl.multiple_of(k * cr, 16), cr)

    def pair0(i):
        k = yo(order[i])
        return remote(
            rec.at[0, 0, :, rows_of(k), pl.ds(pl.multiple_of(d * 512, 256), 256)],
            part.at[0, :, rows_of(k), :], pair_s.at[0, i], pair_r.at[0, i], partner,
        )

    def pair1(i, to_fac):
        k = yo(order[i])
        if to_fac:
            src = fac.at[0, 0, :, rows_of(k), :]
        else:
            src = rec.at[0, 0, :, rows_of(k), pl.ds(256, 256)]
        return remote(src, part.at[1, :, rows_of(k), :], pair_s.at[1, i], pair_r.at[1, i], partner)

    chc = remote(chg, chp, chp_s, chp_r, partner)
    for i in range(ny):
        pair0(i).start()

        @pl.when(d == 1)
        def _():
            pair1(i, True).start()

        @pl.when(d == 0)
        def _():
            pair1(i, False).start()

        if i == 0:
            chc.start()

    own0.wait()
    pltpu.make_async_copy(fac.at[0, 0], own.at[1], own_sem.at[1]).wait()
    chc.wait_recv()

    def chip_sum(i):
        k = yo(order[i])
        pair0(i).wait_recv()
        pair1(i, True).wait_recv()
        for h in range(2):
            r = rows_of(k)
            s = (own[h, 0, r, :].astype(f32) + own[h, 1, r, :].astype(f32)) + (
                part[h, 0, r, :].astype(f32) + part[h, 1, r, :].astype(f32)
            )
            acc[k, h, 0:cr, :] = s
        r8 = pl.ds(pl.multiple_of(k * nz, nz), nz)
        acc[k, 0, cr : cr + nz, :] = chg[r8, :] + chp[r8, :]

    def nrow(h):
        return cr + nz if h == 0 else cr

    def rs(st, s):
        dirn, h = STREAMS[st]
        r = pl.ds(0, nrow(h))
        return remote(
            acc.at[yo(dirn * (half - s)), h, r, :], rbuf.at[st, s, r, :],
            rs_s.at[st, s], rs_r.at[st, s], at(yo(dirn), z, c, x),
        )

    chip_sum(0)
    rs(0, 0).start()
    rs(2, 0).start()
    done = 1
    for s in range(1, half):
        chip_sum(done)
        if s == 1:
            rs(1, 1).start()
        chip_sum(done + 1)
        if s == 1:
            rs(3, 1).start()
        done += 2
        for st in (0, 2, 1, 3):
            if s == 1 and not LONG[st]:
                continue
            dirn, h = STREAMS[st]
            rs(st, s - 1).wait_recv()
            k = yo(dirn * (half - s))
            acc[k, h, 0 : nrow(h), :] += rbuf[st, s - 1, 0 : nrow(h), :]
            rs(st, s).start()
    chip_sum(done)
    zs[:, 8:16, :] = jnp.zeros((nz, 8, 512), f32)
    for h, sts in ((0, (0, 3)), (1, (2, 1))):
        for st in sts:
            rs(st, half - 1).wait_recv()
        n = nrow(h)
        acc[y, h, 0:n, :] = acc[y, h, 0:n, :] + (
            rbuf[sts[0], half - 1, 0:n, :] + rbuf[sts[1], half - 1, 0:n, :]
        )
        for zz in range(nz):
            zs[zz, 0:12, h * 256 : (h + 1) * 256] = acc[y, h, 12 * zz : 12 * zz + 12, :]
            if h == 0:
                zs[zz, 12:13, 0:256] = acc[y, 0, cr + zz : cr + zz + 1, :]

    far = sorted(range(1, nz), key=lambda o: -min(o, nz - o))

    def zc(o):
        return remote(zs.at[zo(o)], zr.at[o - 1], z_s.at[o - 1], z_r.at[o - 1], at(y, zo(o), c, x))

    for o in far:
        zc(o).start()
    total = zs[z]
    for o in reversed(far):
        zc(o).wait_recv()
        total = total + zr[o - 1]
    xb[x] = total

    def xc(o):
        return remote(xb.at[x], xb.at[x], x_s.at[o - 1], x_r.at[o - 1], at(y, z, c, xo(o)))

    for o in range(1, nx):
        xc(o).start()
    for o in range(1, nx):
        xc(o).wait_recv()
    total = xb[0]
    for o in range(1, nx):
        total = total + xb[o]
    sb[...] = total

    low = sb[0:6, :]
    high = sb[6:12, :]
    mine = jnp.where(c == 0, low, high)
    sws[0:6, :] = jnp.where(c == 0, high, low)
    sws[6:8, :] = jnp.zeros((2, 512), f32)
    swap = remote(sws, swr, sw_sem.at[0], sw_sem.at[1], partner)
    swap.start()

    my_ch = jnp.where(c == 0, sb[12:13, 0:128], sb[12:13, 128:256])
    sq = sb[0:8, :] * sb[0:8, :]
    sq = sq[:, 0:128] + sq[:, 128:256] + (sq[:, 256:384] + sq[:, 384:512])
    sh = sb[8:16, :] * sb[8:16, :]
    sh = sh[:, 0:128] + sh[:, 128:256] + (sh[:, 256:384] + sh[:, 384:512])
    row = lax.broadcasted_iota(jnp.int32, (8, 128), 0)
    sh = jnp.where(row < 4, sh, 0.0)
    ch_sq = jnp.where(row == 0, jnp.broadcast_to(my_ch * my_ch, (8, 128)), 0.0)
    n1[0] = sq + sh + ch_sq

    def n1c(o, e):
        i = 2 * o + e
        dev = at(y, zo(o), c if e == 0 else d, x)
        return remote(n1.at[0], n1.at[i], n1_s.at[i], n1_r.at[i], dev)

    n1_list = [(o, e) for o in [*far, 0] for e in range(2) if (o, e) != (0, 0)]
    for o, e in n1_list:
        n1c(o, e).start()
    for o, e in n1_list:
        n1c(o, e).wait_recv()
    part_sum = n1[0]
    for i in range(1, 2 * nz):
        part_sum = part_sum + n1[i]
    n2[0] = part_sum

    def n2c(o):
        return remote(n2.at[0], n2.at[o], n2_s.at[o], n2_r.at[o], at(yo(o), z, c, x))

    for o in range(1, ny):
        n2c(o).start()
    swap.wait_recv()
    for o in range(1, ny):
        n2c(o).wait_recv()
    part_sum = n2[0]
    for o in range(1, ny):
        part_sum = part_sum + n2[o]
    square_sum = jnp.sum(jnp.sum(part_sum, axis=1, keepdims=True), axis=0, keepdims=True)
    clip = jnp.minimum(1.0, max_norm / (jnp.sqrt(square_sum) + norm_eps))

    theirs = swr[0:6, :]
    gl = clip * jnp.where(c == 0, mine, theirs)
    gr = clip * jnp.where(c == 0, theirs, mine)
    nm, nf, ns = adam(gl, mrec[:, 0:512], frec[:, 0:512], srec[:, 0:512], weight_decay_rate)
    omrec[:, 0:512] = nm
    ofrec[:, 0:512] = nf
    osrec[:, 0:512] = ns
    hb[0, 0:6, :] = nm
    nm, nf, ns = adam(
        gr[:, 0:256], mrec[:, 512:768], frec[:, 512:768], srec[:, 512:768], weight_decay_rate
    )
    omrec[:, 512:768] = nm
    ofrec[:, 512:768] = nf
    osrec[:, 512:768] = ns
    hb[1, 0:6, 0:256] = nm
    nm, nf, ns = adam(gr[:, 256:512], mfac[...], ffac[...], sfac[...], weight_decay_rate)
    omfac[...] = nm
    offac[...] = nf
    osfac[...] = ns
    hb[1, 0:6, 256:512] = nm
    nm, nf, ns = adam(clip * my_ch, chs[0:1, :], chs[1:2, :], chs[2:3, :], 0.0)
    och[0:1, :] = nm
    och[1:2, :] = nf
    och[2:3, :] = ns
    for h in range(2):
        hb[h, 6:8, :] = jnp.zeros((2, 512), f32)
        hb[h, 6:7, 0:128] = nm

    aswap = remote(hb.at[d], ar, ag_sem.at[0], ag_sem.at[1], partner)
    aswap.start()
    bb[8:16, :] = jnp.zeros((8, 512), f32)
    asm[cr : cr + 16, :] = jnp.zeros((16, 512), f32)
    aswap.wait_recv()
    kept = hb[c]
    got = ar[...]
    r0 = jnp.where(c == 0, kept, got)
    r1 = jnp.where(c == 0, got, kept)
    bb[0:6, :] = r0[0:6, :]
    bb[6:12, :] = r1[0:6, :]
    bb[12:13, 0:128] = r0[6:7, 0:128]
    bb[12:13, 128:256] = r1[6:7, 0:128]
    zag[z] = bb[...].astype(bf16)

    def zg(o):
        return remote(zag.at[z], zag.at[z], zag_s.at[o - 1], zag_r.at[o - 1], at(y, zo(o), c, x))

    for o in far:
        zg(o).start()
    for o in reversed(far):
        zg(o).wait_recv()
    for zz in range(nz):
        blk = zag[zz].astype(f32)
        asm[12 * zz : 12 * zz + 12, :] = blk[0:12, :]
        asm[cr + zz : cr + zz + 1, 0:256] = blk[12:13, 0:256]
    w[c, y, 0] = asm[:, 0:256].astype(bf16)
    w[c, y, 1] = asm[:, 256:512].astype(bf16)

    def grow(h):
        return cr + 16 if h == 0 else cr

    def yg(st, s):
        dirn, h = STREAMS[st]
        blk = w.at[c, yo(-dirn * s), h, pl.ds(0, grow(h)), :]
        return remote(blk, blk, yag_s.at[st, s], yag_r.at[st, s], at(yo(dirn), z, c, x))

    def to_partner(k, h, ss, rr):
        blk = w.at[c, k, h, pl.ds(0, cr), :]
        return remote(blk, blk, ss, rr, partner)

    def pc(st, s):
        dirn, h = STREAMS[st]
        return to_partner(yo(-dirn * (s + 1)), h, pc_s.at[st, s], pc_r.at[st, s])

    def po(h):
        return to_partner(y, h, po_s.at[h], po_r.at[h])

    steps = [half if v else half - 1 for v in LONG]
    for st in (0, 2, 1, 3):
        yg(st, 0).start()
    po(0).start()
    po(1).start()
    for s in range(half):
        for st in (0, 2, 1, 3):
            if s < steps[st]:
                yg(st, s).wait_recv()
                if s + 1 < steps[st]:
                    yg(st, s + 1).start()
                pc(st, s).start()
    for h in range(2):
        po(h).wait_recv()
    for st in range(4):
        for s in range(steps[st]):
            pc(st, s).wait_recv()
    for k in range(ny):
        r = slice(cr * k, cr * k + cr)
        wrec[r, 0:256] = w[0, k, 0, 0:cr, :]
        wrec[r, 256:512] = w[0, k, 1, 0:cr, :]
        wrec[r, 512:768] = w[1, k, 0, 0:cr, :]
        wfac[r, :] = w[1, k, 1, 0:cr, :]
        wch[nz * k : nz * k + nz, :] = w[c, k, 0, cr : cr + 16, :].astype(f32)[0:nz, :]

    for i in range(ny):
        pair0(i).wait_send()
        pair1(i, True).wait_send()
    chc.wait_send()
    for st in range(4):
        for s in range(0 if LONG[st] else 1, half):
            rs(st, s).wait_send()
        for s in range(steps[st]):
            yg(st, s).wait_send()
            pc(st, s).wait_send()
    for o in range(1, nz):
        zc(o).wait_send()
        zg(o).wait_send()
    for o in range(1, nx):
        xc(o).wait_send()
    for o, e in n1_list:
        n1c(o, e).wait_send()
    for o in range(1, ny):
        n2c(o).wait_send()
    swap.wait_send()
    aswap.wait_send()
    for h in range(2):
        po(h).wait_send()


def body(ny, nz, nx, rec, fac, chan, mrec, mfac, mch, frec, ffac, fch, srec, sfac, sch):
    cr = 12 * nz
    rows = cr * ny
    sd = jax.ShapeDtypeStruct
    chg = jnp.sum(chan, axis=(0, 1, 2), dtype=f32).reshape(ny * nz, 2, 96)
    chg = jnp.pad(chg, ((0, 0), (0, 0), (0, 32))).reshape(ny * nz, 256)
    chs = jnp.pad(jnp.stack([mch, fch, sch]).reshape(3, 96), ((0, 0), (0, 32)))
    vm = pl.BlockSpec(memory_space=pltpu.VMEM)
    hbm = pl.BlockSpec(memory_space=pl.ANY)
    dma = pltpu.SemaphoreType.DMA
    half = ny // 2
    V = pltpu.VMEM
    out = pl.pallas_call(
        functools.partial(kernel, ny, nz, nx),
        out_shape=(
            sd((rows, 768), bf16), sd((rows, 256), bf16), sd((ny * nz, 256), f32),
            sd((6, 768), f32), sd((6, 256), f32), sd((6, 768), f32), sd((6, 256), f32),
            sd((6, 768), f32), sd((6, 256), f32), sd((3, 128), f32),
        ),
        in_specs=[hbm, hbm] + [vm] * 8,
        out_specs=(vm,) * 10,
        scratch_shapes=[
            V((2, 2, rows, 256), bf16), V((2, 2, rows, 256), bf16), V((ny * nz, 256), f32),
            V((ny, 2, cr + nz, 256), f32), V((4, half, cr + nz, 256), f32),
            V((nz, 16, 512), f32), V((nz - 1, 16, 512), f32), V((nx, 16, 512), f32),
            V((16, 512), f32), V((8, 512), f32), V((8, 512), f32),
            V((2 * nz, 8, 128), f32), V((ny, 8, 128), f32), V((2, 8, 512), f32), V((8, 512), f32),
            V((16, 512), f32), V((nz, 16, 512), bf16), V((cr + 16, 512), f32),
            V((2, ny, 2, cr + 16, 256), bf16),
            dma((2,)), dma((2, ny)), dma((2, ny)), dma, dma,
            dma((4, half)), dma((4, half)), dma((nz - 1,)), dma((nz - 1,)),
            dma((nx - 1,)), dma((nx - 1,)), dma((2,)),
            dma((2 * nz,)), dma((2 * nz,)), dma((ny,)), dma((ny,)), dma((2,)),
            dma((nz - 1,)), dma((nz - 1,)), dma((4, half)), dma((4, half)),
            dma((4, half)), dma((4, half)), dma((2,)), dma((2,)),
        ],
        compiler_params=pltpu.CompilerParams(
            collective_id=0, has_side_effects=True, vmem_limit_bytes=48 << 20
        ),
    )(rec, fac, chg, mrec, mfac, frec, ffac, srec, sfac, chs)
    wrec, wfac, wch, omrec, omfac, ofrec, offac, osrec, osfac, och = out
    wch = wch.reshape(ny * nz, 2, 128)[:, :, :96].reshape(rows, 16).astype(bf16)
    och = och[:, :96].reshape(3, 6, 16)
    return (
        wrec, wfac, wch,
        omrec, omfac, och[0],
        ofrec, offac, och[1],
        osrec, osfac, och[2],
    )


def solution(mesh, nz=NZ):
    nx = mesh.shape["rep"]
    ny = mesh.shape["dp"] // (2 * nz)
    grad = P("dp", "rep", None, None, None)
    row = P("dp", None)
    return jax.shard_map(
        functools.partial(body, ny, nz, nx),
        mesh=mesh,
        in_specs=(grad,) * 3 + (row,) * 9,
        out_specs=(P(),) * 3 + (row,) * 9,
        check_vma=False,
    )
```

time: 403 us -> 96.4 us (0.24)
  waiting for transfers between devices: 369 us -> 0 us
  Pallas kernels: 0 us -> 81.7 us
  between operations: 14.9 us -> 0.83 us
  other arithmetic: 13.4 us -> 0.83 us
  local copies, waits for them, and re-layouts: 5.78 us -> 12.8 us
    psum x1 -> x0, waiting for transfers between devices: 288 us -> none  [body(): full_sum = lax.psum(local_sum, ('dp', 'rep'))]
    pallas_call x0 -> x1, Pallas kernels: none -> 81.7 us  [body(): pl.pallas_call(functools.partial(kernel, ny, nz, nx), out_shape=(sd((rows...]
    all_gather x1 -> x0, waiting for transfers between devices: 80.3 us -> none  [body(): collected_parts = lax.all_gather(packed_gradients, 'dp', axis=0, tiled=True)]
    reduce_sum x4 -> x1, other arithmetic: 7.97 us -> 0.81 us  [body(): chg = jnp.sum(chan, axis=(0, 1, 2), dtype=f32).reshape(ny * nz, 2, 96)]
    unnamed x20 -> x26, local copies, waits for them, and re-layouts: 3.75 us -> 7.8 us
  transfers between devices with their start and end apart: 2 -> 0, of which waited for: 2 -> 0; matrix products, arithmetic and copies ran while one was open for 0% -> 0% of each run, Pallas kernels for 0% -> 0%
where the time goes in v1:
time: 96.4 us; the launch traced here: 96.1 us
  Pallas kernels  81.7 us (85%)
  local copies, waits for them, and re-layouts  12.8 us (13%)
    pallas_call x1, Pallas kernels, body(): pl.pallas_call(functools.partial(kernel, ny, nz, nx), out_shape=(sd((rows...  81.7 us
    unnamed x26, local copies, waits for them, and re-layouts  7.8 us
    another operation x3, local copies, waits for them, and re-layouts, body(): chs = jnp.pad(jnp.stack([mch, fch, sch]).reshape(3, 96), ((0, 0), (0, 32)))  2.37 us

profile of v1, /device:TPU:1, one launch (start us, length us, event | category | flops | bytes accessed | tf_op | source)
XLA Modules:
  0.0 96.1 jit_solution(4348927088103642175)
XLA Ops:
  0.6 0.0 copy-start.7
  0.7 0.0 copy-start.4
  0.7 0.0 copy-start.6
  0.7 0.0 copy-start.3
  0.7 0.0 copy-start.5
  0.7 0.0 copy-start.2
  0.7 0.0 copy-start.1
  0.7 0.8 stack.12
  1.6 0.8 stack.13
  2.3 0.8 stack.14
  3.1 0.8 convert_reduce_fusion
  3.9 0.2 copy.25
  4.1 0.2 reshape.50
  4.3 0.0 copy-done.7
  4.3 0.0 copy-done.4
  4.3 0.0 copy-done.6
  4.3 0.0 copy-done.3
  4.4 0.0 copy-done.5
  4.4 0.0 copy-done.2
  4.4 0.0 copy-done.1
  4.4 0.0 copy-start
  4.4 1.7 %copy-done = bf16[1,1,2,768,768]{4,3,2,1,0:T(8,128)(2,1)S(1)} copy-done((bf16[1,1,2,768,768]{4,3,2,1,0:T(8,128)(2,1)S(1)}, bf16[1,1,2,768,768]{4,3,2,1,0:T(8,128)(2,1)}, u32[]{:S(2)}) %copy-start) | copy-done | bytes 2359320
  6.1 81.7 %shard_map.211 = (bf16[768,768]{1,0:T(8,128)(2,1)S(1)}, bf16[768,256]{1,0:T(8,128)(2,1)S(1)}, f32[64,256]{1,0:T(8,128)S(1)}, f32[6,768]{1,0:T(8,128)S(1)}, f32[6...) custom-call(bf16[1,1,2,768,768]{4,3,2,1,0:T(8,128)(2,1)S(1)} %copy-d, ...), custom_call_target="tpu_custom_call" | custom-call | tf_op jit(solution)/shard_map/pallas_call | solution.py:412
  87.8 0.7 squeeze.11
  88.4 0.7 squeeze.10
  89.1 0.7 squeeze.9
  89.8 0.2 convert_element_type.12
  90.0 0.7 copy.26
  90.7 1.0 %copy.38 = bf16[768,768]{1,0:T(8,128)(2,1)} copy(bf16[768,768]{1,0:T(8,128)(2,1)S(1)} %get-tuple-element.71) | data formatting | bytes 2359296
  91.7 0.7 copy.39
  92.5 0.6 copy.40
  93.1 0.6 copy.41
  93.7 0.6 copy.42
  94.3 0.6 copy.43
  94.9 0.6 copy.44
  95.5 0.6 copy.45
  (6 shorter events, 0.1 us)
Async XLA Ops:
  0.6 3.7 %copy-start.7 = (f32[6,256]{1,0:T(8,128)S(1)}, f32[6,256]{1,0:T(8,128)}, u32[]{:S(2)}) copy-start(f32[6,256]{1,0:T(8,128)} %sfac.1) | copy-start | bytes 18436
  0.7 3.7 %copy-start.4 = (f32[6,768]{1,0:T(8,128)S(1)}, f32[6,768]{1,0:T(8,128)}, u32[]{:S(2)}) copy-start(f32[6,768]{1,0:T(8,128)} %srec.1) | copy-start | bytes 55300
  0.7 3.7 %copy-start.6 = (f32[6,256]{1,0:T(8,128)S(1)}, f32[6,256]{1,0:T(8,128)}, u32[]{:S(2)}) copy-start(f32[6,256]{1,0:T(8,128)} %ffac.1) | copy-start | bytes 18436
  0.7 3.7 %copy-start.3 = (f32[6,768]{1,0:T(8,128)S(1)}, f32[6,768]{1,0:T(8,128)}, u32[]{:S(2)}) copy-start(f32[6,768]{1,0:T(8,128)} %frec.1) | copy-start | bytes 55300
  0.7 3.7 %copy-start.5 = (f32[6,256]{1,0:T(8,128)S(1)}, f32[6,256]{1,0:T(8,128)}, u32[]{:S(2)}) copy-start(f32[6,256]{1,0:T(8,128)} %mfac.1) | copy-start | bytes 18436
  0.7 3.7 %copy-start.2 = (f32[6,768]{1,0:T(8,128)S(1)}, f32[6,768]{1,0:T(8,128)}, u32[]{:S(2)}) copy-start(f32[6,768]{1,0:T(8,128)} %mrec.1) | copy-start | bytes 55300
  0.7 3.7 %copy-start.1 = (bf16[1,1,2,768,256]{4,3,2,1,0:T(8,128)(2,1)S(1)}, bf16[1,1,2,768,256]{4,3,2,1,0:T(8,128)(2,1)}, u32[]{:S(2)}) copy-start(bf16[1,1,2,768,256]{4,3,2,1,0:T(8,128)(2,1)} %fac.1) | copy-start | bytes 2359300
  4.4 1.7 %copy-start = (bf16[1,1,2,768,768]{4,3,2,1,0:T(8,128)(2,1)S(1)}, bf16[1,1,2,768,768]{4,3,2,1,0:T(8,128)(2,1)}, u32[]{:S(2)}) copy-start(bf16[1,1,2,768,768]{4,3,2,1,0:T(8,128)(2,1)} %rec.1) | copy-start | bytes 7077892

commit v2 on v1

--- a/solution.py
+++ b/solution.py
@@ -40,9 +40,9 @@
 
 def kernel(
     ny, nz, nx,
-    rec, fac, chg, mrec, mfac, frec, ffac, srec, sfac, chs,
-    wrec, wfac, wch, omrec, omfac, ofrec, offac, osrec, osfac, och,
-    own, part, chp, acc, rbuf, zs, zr, xb, sb, sws, swr, n1, n2, hb, ar, bb, zag, asm, w,
+    rec, fac, chg, mrec, mfac, mch, frec, ffac, fch, srec, sfac, sch,
+    wrec, wfac, wch, omrec, omfac, omch, ofrec, offac, ofch, osrec, osfac, osch,
+    chs, och, own, part, chp, acc, rbuf, zs, zr, xb, sb, sws, swr, n1, n2, hb, ar, bb, zag, asm, w,
     own_sem, pair_s, pair_r, chp_s, chp_r, rs_s, rs_r, z_s, z_r, x_s, x_r, sw_sem,
     n1_s, n1_r, n2_s, n2_r, ag_sem, zag_s, zag_r, yag_s, yag_r, pc_s, pc_r, po_s, po_r,
 ):
@@ -97,6 +97,10 @@
         peers.append(at(y, z, c, xo(o)))
     for dev in peers:
         pl.semaphore_signal(barrier, inc=1, device_id=dev, device_id_type=MESH)
+    chs[...] = jnp.zeros_like(chs)
+    for i, ref in enumerate((mch, fch, sch)):
+        for r in range(6):
+            chs[i : i + 1, 16 * r : 16 * r + 16] = ref[r : r + 1, :]
     pl.semaphore_wait(barrier, len(peers))
 
     order = [half]
@@ -319,6 +323,9 @@
 
     for o in far:
         zg(o).start()
+    for i, ref in enumerate((omch, ofch, osch)):
+        for r in range(6):
+            ref[r : r + 1, :] = och[i : i + 1, 16 * r : 16 * r + 16]
     for o in reversed(far):
         zg(o).wait_recv()
     for zz in range(nz):
@@ -397,15 +404,26 @@
         po(h).wait_send()
 
 
+def write_out(*refs):
+    n = (len(refs) - 1) // 2
+    sem = refs[-1]
+    copies = [
+        pltpu.make_async_copy(refs[i], refs[n + i], sem.at[i]) for i in range(n)
+    ]
+    for copy in copies:
+        copy.start()
+    for copy in copies:
+        copy.wait()
+
+
 def body(ny, nz, nx, rec, fac, chan, mrec, mfac, mch, frec, ffac, fch, srec, sfac, sch):
     cr = 12 * nz
     rows = cr * ny
     sd = jax.ShapeDtypeStruct
     chg = jnp.sum(chan, axis=(0, 1, 2), dtype=f32).reshape(ny * nz, 2, 96)
     chg = jnp.pad(chg, ((0, 0), (0, 0), (0, 32))).reshape(ny * nz, 256)
-    chs = jnp.pad(jnp.stack([mch, fch, sch]).reshape(3, 96), ((0, 0), (0, 32)))
     vm = pl.BlockSpec(memory_space=pltpu.VMEM)
-    hbm = pl.BlockSpec(memory_space=pl.ANY)
+    hbm = pl.BlockSpec(memory_space=pltpu.HBM)
     dma = pltpu.SemaphoreType.DMA
     half = ny // 2
     V = pltpu.VMEM
@@ -413,12 +431,12 @@
         functools.partial(kernel, ny, nz, nx),
         out_shape=(
             sd((rows, 768), bf16), sd((rows, 256), bf16), sd((ny * nz, 256), f32),
-            sd((6, 768), f32), sd((6, 256), f32), sd((6, 768), f32), sd((6, 256), f32),
-            sd((6, 768), f32), sd((6, 256), f32), sd((3, 128), f32),
-        ),
-        in_specs=[hbm, hbm] + [vm] * 8,
-        out_specs=(vm,) * 10,
+        )
+        + (sd((6, 768), f32), sd((6, 256), f32), sd((6, 16), f32)) * 3,
+        in_specs=[hbm, hbm] + [vm] * 10,
+        out_specs=(vm,) * 12,
         scratch_shapes=[
+            V((8, 128), f32), V((8, 128), f32),
             V((2, 2, rows, 256), bf16), V((2, 2, rows, 256), bf16), V((ny * nz, 256), f32),
             V((ny, 2, cr + nz, 256), f32), V((4, half, cr + nz, 256), f32),
             V((nz, 16, 512), f32), V((nz - 1, 16, 512), f32), V((nx, 16, 512), f32),
@@ -434,18 +452,20 @@
             dma((4, half)), dma((4, half)), dma((2,)), dma((2,)),
         ],
         compiler_params=pltpu.CompilerParams(
-            collective_id=0, has_side_effects=True, vmem_limit_bytes=48 << 20
+            collective_id=0, has_side_effects=True, vmem_limit_bytes=48_000_000
         ),
-    )(rec, fac, chg, mrec, mfac, frec, ffac, srec, sfac, chs)
-    wrec, wfac, wch, omrec, omfac, ofrec, offac, osrec, osfac, och = out
-    wch = wch.reshape(ny * nz, 2, 128)[:, :, :96].reshape(rows, 16).astype(bf16)
-    och = och[:, :96].reshape(3, 6, 16)
-    return (
-        wrec, wfac, wch,
-        omrec, omfac, och[0],
-        ofrec, offac, och[1],
-        osrec, osfac, och[2],
-    )
+    )(rec, fac, chg, mrec, mfac, mch, frec, ffac, fch, srec, sfac, sch)
+    wch = out[2].reshape(ny * nz, 2, 128)[:, :, :96].reshape(rows, 16).astype(bf16)
+    held = out[:2] + out[3:]
+    final = pl.pallas_call(
+        write_out,
+        out_shape=tuple(sd(o.shape, o.dtype) for o in held),
+        in_specs=[pl.BlockSpec(memory_space=pl.ANY)] * len(held),
+        out_specs=(pl.BlockSpec(memory_space=pl.ANY),) * len(held),
+        scratch_shapes=[dma((len(held),))],
+        compiler_params=pltpu.CompilerParams(vmem_limit_bytes=1 << 20),
+    )(*held)
+    return (final[0], final[1], wch, *final[2:])
 
 
 def solution(mesh, nz=NZ):

time: 96.4 us -> 88 us (0.913)
  local copies, waits for them, and re-layouts: 12.8 us -> 2.98 us
  Pallas kernels: 81.7 us -> 83 us
    unnamed x26 -> x24, local copies, waits for them, and re-layouts: 7.8 us -> 2.44 us
    another operation x3 -> x0, local copies, waits for them, and re-layouts: 2.37 us -> none  [body(): chs = jnp.pad(jnp.stack([mch, fch, sch]).reshape(3, 96), ((0, 0), (0, 32)))]
    squeeze x3 -> x0, local copies, waits for them, and re-layouts: 2.01 us -> none  [the longest x1 0.67 us: body(): och[2]]
    pallas_call x0 -> x1, Pallas kernels: none -> 1.27 us  [body(): pl.pallas_call(write_out, out_shape=tuple((sd(o.shape, o.dtype) for o in...]
where the time goes in v2:
time: 88 us; the launch traced here: 87.8 us
  Pallas kernels  83 us (94%)
  local copies, waits for them, and re-layouts  2.98 us (3%)
  other arithmetic  0.89 us (1%)
  between operations  0.88 us (1%)
    pallas_call x1, Pallas kernels, body(): pl.pallas_call(functools.partial(kernel, ny, nz, nx), out_shape=(sd((rows...  81.8 us
    unnamed x24, local copies, waits for them, and re-layouts  2.44 us

profile of v2, /device:TPU:1, one launch (start us, length us, event | category | flops | bytes accessed | tf_op | source)
XLA Modules:
  0.0 87.8 jit_solution(1689304502901237682)
XLA Ops:
  0.6 0.0 copy-start.10
  0.7 0.0 copy-start.7
  0.7 0.0 copy-start.4
  0.7 0.0 copy-start.9
  0.7 0.0 copy-start.6
  0.7 0.0 copy-start.3
  0.7 0.0 copy-start.8
  0.7 0.0 copy-start.5
  0.7 0.0 copy-start.2
  0.7 0.0 copy-start.1
  0.7 0.9 %convert_reduce_fusion = f32[768,16]{0,1:T(8,128)S(1)} fusion(bf16[1,1,2,768,16]{3,4,2,1,0:T(8,128)(2,1)} %param.14), kind=kLoop, calls=%fused_computation | loop fusion | flops 36864 | bytes 98304 | tf_op jit(solution)/shard_map/reduce_sum | solution.py:423
  1.6 0.2 copy.25
  1.8 0.2 reshape.36
  2.0 0.0 copy-done.10
  2.0 0.0 copy-done.7
  2.1 0.0 copy-done.4
  2.1 0.0 copy-done.9
  2.1 0.0 copy-done.6
  2.1 0.0 copy-done.3
  2.1 0.0 copy-done.8
  2.1 0.0 copy-done.5
  2.1 0.0 copy-done.2
  2.1 0.0 copy-done.1
  2.1 0.0 copy-start
  2.1 1.7 %copy-done = bf16[1,1,2,768,768]{4,3,2,1,0:T(8,128)(2,1)S(1)} copy-done((bf16[1,1,2,768,768]{4,3,2,1,0:T(8,128)(2,1)S(1)}, bf16[1,1,2,768,768]{4,3,2,1,0:T(8,128)(2,1)}, u32[]{:S(2)}) %copy-start) | copy-done | bytes 2359320
  3.8 81.8 %shard_map.211 = (bf16[768,768]{1,0:T(8,128)(2,1)S(1)}, bf16[768,256]{1,0:T(8,128)(2,1)S(1)}, f32[64,256]{1,0:T(8,128)S(1)}, f32[6,768]{1,0:T(8,128)S(1)}, f32[6...) custom-call(bf16[1,1,2,768,768]{4,3,2,1,0:T(8,128)(2,1)S(1)} %copy-d, ...), custom_call_target="tpu_custom_call" | custom-call | tf_op jit(solution)/shard_map/pallas_call | solution.py:430
  85.6 1.3 %shard_map.212 = (bf16[768,768]{1,0:T(8,128)(2,1)}, bf16[768,256]{1,0:T(8,128)(2,1)}, f32[6,768]{1,0:T(8,128)}, f32[6,256]{1,0:T(8,128)}, f32[6,16]{1,0:T(8,128)...) custom-call(bf16[768,768]{1,0:T(8,128)(2,1)S(1)} %get-tuple-element., ...), custom_call_target="tpu_custom_call" | custom-call | tf_op jit(solution)/shard_map/pallas_call | solution.py:460
  86.9 0.2 convert_element_type.10
  87.1 0.7 copy.26
  (4 shorter events, 0.1 us)
Async XLA Ops:
  0.6 1.4 %copy-start.10 = (f32[6,16]{1,0:T(8,128)S(1)}, f32[6,16]{1,0:T(8,128)}, u32[]{:S(2)}) copy-start(f32[6,16]{1,0:T(8,128)} %sch.1) | copy-start | bytes 1156
  0.7 1.4 %copy-start.7 = (f32[6,256]{1,0:T(8,128)S(1)}, f32[6,256]{1,0:T(8,128)}, u32[]{:S(2)}) copy-start(f32[6,256]{1,0:T(8,128)} %sfac.1) | copy-start | bytes 18436
  0.7 1.4 %copy-start.4 = (f32[6,768]{1,0:T(8,128)S(1)}, f32[6,768]{1,0:T(8,128)}, u32[]{:S(2)}) copy-start(f32[6,768]{1,0:T(8,128)} %srec.1) | copy-start | bytes 55300
  0.7 1.4 %copy-start.9 = (f32[6,16]{1,0:T(8,128)S(1)}, f32[6,16]{1,0:T(8,128)}, u32[]{:S(2)}) copy-start(f32[6,16]{1,0:T(8,128)} %fch.1) | copy-start | bytes 1156
  0.7 1.4 %copy-start.6 = (f32[6,256]{1,0:T(8,128)S(1)}, f32[6,256]{1,0:T(8,128)}, u32[]{:S(2)}) copy-start(f32[6,256]{1,0:T(8,128)} %ffac.1) | copy-start | bytes 18436
  0.7 1.4 %copy-start.3 = (f32[6,768]{1,0:T(8,128)S(1)}, f32[6,768]{1,0:T(8,128)}, u32[]{:S(2)}) copy-start(f32[6,768]{1,0:T(8,128)} %frec.1) | copy-start | bytes 55300
  0.7 1.4 %copy-start.8 = (f32[6,16]{1,0:T(8,128)S(1)}, f32[6,16]{1,0:T(8,128)}, u32[]{:S(2)}) copy-start(f32[6,16]{1,0:T(8,128)} %mch.1) | copy-start | bytes 1156
  0.7 1.4 %copy-start.5 = (f32[6,256]{1,0:T(8,128)S(1)}, f32[6,256]{1,0:T(8,128)}, u32[]{:S(2)}) copy-start(f32[6,256]{1,0:T(8,128)} %mfac.1) | copy-start | bytes 18436
  0.7 1.4 %copy-start.2 = (f32[6,768]{1,0:T(8,128)S(1)}, f32[6,768]{1,0:T(8,128)}, u32[]{:S(2)}) copy-start(f32[6,768]{1,0:T(8,128)} %mrec.1) | copy-start | bytes 55300
  0.7 1.4 %copy-start.1 = (bf16[1,1,2,768,256]{4,3,2,1,0:T(8,128)(2,1)S(1)}, bf16[1,1,2,768,256]{4,3,2,1,0:T(8,128)(2,1)}, u32[]{:S(2)}) copy-start(bf16[1,1,2,768,256]{4,3,2,1,0:T(8,128)(2,1)} %fac.1) | copy-start | bytes 2359300
  2.1 1.7 %copy-start = (bf16[1,1,2,768,768]{4,3,2,1,0:T(8,128)(2,1)S(1)}, bf16[1,1,2,768,768]{4,3,2,1,0:T(8,128)(2,1)}, u32[]{:S(2)}) copy-start(bf16[1,1,2,768,768]{4,3,2,1,0:T(8,128)(2,1)} %rec.1) | copy-start | bytes 7077892

commit v3 on v2

--- a/solution.py
+++ b/solution.py
@@ -42,8 +42,8 @@
     ny, nz, nx,
     rec, fac, chg, mrec, mfac, mch, frec, ffac, fch, srec, sfac, sch,
     wrec, wfac, wch, omrec, omfac, omch, ofrec, offac, ofch, osrec, osfac, osch,
-    chs, och, own, part, chp, acc, rbuf, zs, zr, xb, sb, sws, swr, n1, n2, hb, ar, bb, zag, asm, w,
-    own_sem, pair_s, pair_r, chp_s, chp_r, rs_s, rs_r, z_s, z_r, x_s, x_r, sw_sem,
+    chs, och, own, part, chp, tmp, acc, acz, rbuf, rbuz, zs, zr, ys, yr, xb, sb, sws, swr, n1, n2, hb, ar, bb, zag, asm, w,
+    own_sem, pair_s, pair_r, chp_s, chp_r, rs_s, rs_r, rz_s, rz_r, z_s, z_r, y_s, y_r, x_s, x_r, sw_sem,
     n1_s, n1_r, n2_s, n2_r, ag_sem, zag_s, zag_r, yag_s, yag_r, pc_s, pc_r, po_s, po_r,
 ):
     cr = 12 * nz
@@ -145,76 +145,124 @@
     pltpu.make_async_copy(fac.at[0, 0], own.at[1], own_sem.at[1]).wait()
     chc.wait_recv()
 
+    def pair_sum(h, r):
+        return (own[h, 0, r, :].astype(f32) + own[h, 1, r, :].astype(f32)) + (
+            part[h, 0, r, :].astype(f32) + part[h, 1, r, :].astype(f32)
+        )
+
     def chip_sum(i):
         k = yo(order[i])
         pair0(i).wait_recv()
-        pair1(i, True).wait_recv()
-        for h in range(2):
-            r = rows_of(k)
-            s = (own[h, 0, r, :].astype(f32) + own[h, 1, r, :].astype(f32)) + (
-                part[h, 0, r, :].astype(f32) + part[h, 1, r, :].astype(f32)
-            )
-            acc[k, h, 0:cr, :] = s
+        s = pair_sum(0, rows_of(k))
         r8 = pl.ds(pl.multiple_of(k * nz, nz), nz)
-        acc[k, 0, cr : cr + nz, :] = chg[r8, :] + chp[r8, :]
-
-    def nrow(h):
-        return cr + nz if h == 0 else cr
+        ch = chg[r8, :] + chp[r8, :]
+        for u in range(2):
+            acc[k, u, 0:cr, :] = s[:, 128 * u : 128 * u + 128]
+            acc[k, u, cr : cr + nz, :] = ch[:, 128 * u : 128 * u + 128]
+
+    def chip_sum_z():
+        for i in range(ny):
+            pair1(i, True).wait_recv()
+        for k in range(ny):
+            tmp[k] = pair_sum(1, slice(cr * k, cr * k + cr))
+            for zz in range(nz):
+                for u in range(2):
+                    acz[zz, u, 12 * k : 12 * k + 12, :] = tmp[
+                        k, 12 * zz : 12 * zz + 12, 128 * u : 128 * u + 128
+                    ]
 
     def rs(st, s):
-        dirn, h = STREAMS[st]
-        r = pl.ds(0, nrow(h))
+        dirn, u = STREAMS[st]
         return remote(
-            acc.at[yo(dirn * (half - s)), h, r, :], rbuf.at[st, s, r, :],
+            acc.at[yo(dirn * (half - s)), u], rbuf.at[st, s],
             rs_s.at[st, s], rs_r.at[st, s], at(yo(dirn), z, c, x),
+        )
+
+    def rz(st, s):
+        dirn, u = STREAMS[st]
+        return remote(
+            acz.at[zo(dirn * (half - s) + nz), u], rbuz.at[st, s],
+            rz_s.at[st, s], rz_r.at[st, s], at(y, zo(dirn + nz), c, x),
         )
 
     chip_sum(0)
     rs(0, 0).start()
     rs(2, 0).start()
     done = 1
+    if half > 1:
+        chip_sum(1)
+        rs(1, 1).start()
+        chip_sum(2)
+        rs(3, 1).start()
+        done = 3
+    chip_sum_z()
+    rz(0, 0).start()
+    rz(2, 0).start()
+    if half > 1:
+        rz(1, 1).start()
+        rz(3, 1).start()
     for s in range(1, half):
-        chip_sum(done)
-        if s == 1:
-            rs(1, 1).start()
-        chip_sum(done + 1)
-        if s == 1:
-            rs(3, 1).start()
-        done += 2
         for st in (0, 2, 1, 3):
             if s == 1 and not LONG[st]:
                 continue
-            dirn, h = STREAMS[st]
+            dirn, u = STREAMS[st]
             rs(st, s - 1).wait_recv()
             k = yo(dirn * (half - s))
-            acc[k, h, 0 : nrow(h), :] += rbuf[st, s - 1, 0 : nrow(h), :]
+            acc[k, u] += rbuf[st, s - 1]
             rs(st, s).start()
-    chip_sum(done)
-    zs[:, 8:16, :] = jnp.zeros((nz, 8, 512), f32)
-    for h, sts in ((0, (0, 3)), (1, (2, 1))):
+        while done < min(2 * s + 3, ny):
+            chip_sum(done)
+            done += 1
+        for st in (0, 2, 1, 3):
+            if s == 1 and not LONG[st]:
+                continue
+            dirn, u = STREAMS[st]
+            rz(st, s - 1).wait_recv()
+            k = zo(dirn * (half - s) + nz)
+            acz[k, u] += rbuz[st, s - 1]
+            rz(st, s).start()
+    while done < ny:
+        chip_sum(done)
+        done += 1
+    zs[:, 8:16, :] = jnp.zeros((nz, 8, 256), f32)
+    ys[:, 8:16, :] = jnp.zeros((ny, 8, 256), f32)
+
+    far = sorted(range(1, nz), key=lambda o: -min(o, nz - o))
+
+    def zc(o):
+        return remote(zs.at[zo(o)], zr.at[o - 1], z_s.at[o - 1], z_r.at[o - 1], at(y, zo(o), c, x))
+
+    def yc(o):
+        return remote(ys.at[yo(o)], yr.at[o - 1], y_s.at[o - 1], y_r.at[o - 1], at(yo(o), z, c, x))
+
+    for u, sts in ((0, (0, 3)), (1, (2, 1))):
         for st in sts:
             rs(st, half - 1).wait_recv()
-        n = nrow(h)
-        acc[y, h, 0:n, :] = acc[y, h, 0:n, :] + (
-            rbuf[sts[0], half - 1, 0:n, :] + rbuf[sts[1], half - 1, 0:n, :]
-        )
+        acc[y, u] = acc[y, u] + (rbuf[sts[0], half - 1] + rbuf[sts[1], half - 1])
         for zz in range(nz):
-            zs[zz, 0:12, h * 256 : (h + 1) * 256] = acc[y, h, 12 * zz : 12 * zz + 12, :]
-            if h == 0:
-                zs[zz, 12:13, 0:256] = acc[y, 0, cr + zz : cr + zz + 1, :]
-
-    far = sorted(range(1, nz), key=lambda o: -min(o, nz - o))
-
-    def zc(o):
-        return remote(zs.at[zo(o)], zr.at[o - 1], z_s.at[o - 1], z_r.at[o - 1], at(y, zo(o), c, x))
-
+            lanes = slice(128 * u, 128 * u + 128)
+            zs[zz, 0:12, lanes] = acc[y, u, 12 * zz : 12 * zz + 12, :]
+            zs[zz, 12:13, lanes] = acc[y, u, cr + zz : cr + zz + 1, :]
     for o in far:
         zc(o).start()
+    for u, sts in ((0, (0, 3)), (1, (2, 1))):
+        for st in sts:
+            rz(st, half - 1).wait_recv()
+        acz[z, u] = acz[z, u] + (rbuz[sts[0], half - 1] + rbuz[sts[1], half - 1])
+        for yy in range(ny):
+            ys[yy, 0:12, 128 * u : 128 * u + 128] = acz[z, u, 12 * yy : 12 * yy + 12, :]
+    for o in far:
+        yc(o).start()
     total = zs[z]
     for o in reversed(far):
         zc(o).wait_recv()
         total = total + zr[o - 1]
-    xb[x] = total
+    xb[x, :, 0:256] = total
+    total = ys[y]
+    for o in reversed(far):
+        yc(o).wait_recv()
+        total = total + yr[o - 1]
+    xb[x, :, 256:512] = total
 
     def xc(o):
         return remote(xb.at[x], xb.at[x], x_s.at[o - 1], x_r.at[o - 1], at(y, z, c, xo(o)))
@@ -386,11 +434,13 @@
     for st in range(4):
         for s in range(0 if LONG[st] else 1, half):
             rs(st, s).wait_send()
+            rz(st, s).wait_send()
         for s in range(steps[st]):
             yg(st, s).wait_send()
             pc(st, s).wait_send()
     for o in range(1, nz):
         zc(o).wait_send()
+        yc(o).wait_send()
         zg(o).wait_send()
     for o in range(1, nx):
         xc(o).wait_send()
@@ -438,14 +488,18 @@
         scratch_shapes=[
             V((8, 128), f32), V((8, 128), f32),
             V((2, 2, rows, 256), bf16), V((2, 2, rows, 256), bf16), V((ny * nz, 256), f32),
-            V((ny, 2, cr + nz, 256), f32), V((4, half, cr + nz, 256), f32),
-            V((nz, 16, 512), f32), V((nz - 1, 16, 512), f32), V((nx, 16, 512), f32),
+            V((ny, cr, 256), f32),
+            V((ny, 2, cr + nz, 128), f32), V((nz, 2, cr, 128), f32),
+            V((4, half, cr + nz, 128), f32), V((4, half, cr, 128), f32),
+            V((nz, 16, 256), f32), V((nz - 1, 16, 256), f32),
+            V((ny, 16, 256), f32), V((ny - 1, 16, 256), f32), V((nx, 16, 512), f32),
             V((16, 512), f32), V((8, 512), f32), V((8, 512), f32),
             V((2 * nz, 8, 128), f32), V((ny, 8, 128), f32), V((2, 8, 512), f32), V((8, 512), f32),
             V((16, 512), f32), V((nz, 16, 512), bf16), V((cr + 16, 512), f32),
             V((2, ny, 2, cr + 16, 256), bf16),
             dma((2,)), dma((2, ny)), dma((2, ny)), dma, dma,
-            dma((4, half)), dma((4, half)), dma((nz - 1,)), dma((nz - 1,)),
+            dma((4, half)), dma((4, half)), dma((4, half)), dma((4, half)),
+            dma((nz - 1,)), dma((nz - 1,)), dma((ny - 1,)), dma((ny - 1,)),
             dma((nx - 1,)), dma((nx - 1,)), dma((2,)),
             dma((2 * nz,)), dma((2 * nz,)), dma((ny,)), dma((ny,)), dma((2,)),
             dma((nz - 1,)), dma((nz - 1,)), dma((4, half)), dma((4, half)),
@@ -471,6 +525,7 @@
 def solution(mesh, nz=NZ):
     nx = mesh.shape["rep"]
     ny = mesh.shape["dp"] // (2 * nz)
+    assert ny == nz and ny % 2 == 0
     grad = P("dp", "rep", None, None, None)
     row = P("dp", None)
     return jax.shard_map(

time: 88 us -> 84.6 us (0.961)
  Pallas kernels: 83 us -> 79.7 us
    pallas_call x1, Pallas kernels: 81.8 us -> 78.4 us  [body(): pl.pallas_call(functools.partial(kernel, ny, nz, nx), out_shape=(sd((rows...]
where the time goes in v3:
time: 84.6 us; the launch traced here: 84.4 us
  Pallas kernels  79.7 us (94%)
  local copies, waits for them, and re-layouts  2.98 us (4%)
  other arithmetic  0.89 us (1%)
  between operations  0.88 us (1%)
    pallas_call x1, Pallas kernels, body(): pl.pallas_call(functools.partial(kernel, ny, nz, nx), out_shape=(sd((rows...  78.4 us
    unnamed x24, local copies, waits for them, and re-layouts  2.44 us

profile of v3, /device:TPU:1, one launch (start us, length us, event | category | flops | bytes accessed | tf_op | source)
XLA Modules:
  0.0 84.4 jit_solution(17909070680811459073)
XLA Ops:
  0.6 0.0 copy-start.10
  0.7 0.0 copy-start.7
  0.7 0.0 copy-start.4
  0.7 0.0 copy-start.9
  0.7 0.0 copy-start.6
  0.7 0.0 copy-start.3
  0.7 0.0 copy-start.8
  0.7 0.0 copy-start.5
  0.7 0.0 copy-start.2
  0.7 0.0 copy-start.1
  0.7 0.9 %convert_reduce_fusion = f32[768,16]{0,1:T(8,128)S(1)} fusion(bf16[1,1,2,768,16]{3,4,2,1,0:T(8,128)(2,1)} %param.14), kind=kLoop, calls=%fused_computation | loop fusion | flops 36864 | bytes 98304 | tf_op jit(solution)/shard_map/reduce_sum | solution.py:473
  1.6 0.2 copy.25
  1.8 0.2 reshape.36
  2.0 0.0 copy-done.10
  2.0 0.0 copy-done.7
  2.1 0.0 copy-done.4
  2.1 0.0 copy-done.9
  2.1 0.0 copy-done.6
  2.1 0.0 copy-done.3
  2.1 0.0 copy-done.8
  2.1 0.0 copy-done.5
  2.1 0.0 copy-done.2
  2.1 0.0 copy-done.1
  2.1 0.0 copy-start
  2.1 1.7 %copy-done = bf16[1,1,2,768,768]{4,3,2,1,0:T(8,128)(2,1)S(1)} copy-done((bf16[1,1,2,768,768]{4,3,2,1,0:T(8,128)(2,1)S(1)}, bf16[1,1,2,768,768]{4,3,2,1,0:T(8,128)(2,1)}, u32[]{:S(2)}) %copy-start) | copy-done | bytes 2359320
  3.8 78.4 %shard_map.211 = (bf16[768,768]{1,0:T(8,128)(2,1)S(1)}, bf16[768,256]{1,0:T(8,128)(2,1)S(1)}, f32[64,256]{1,0:T(8,128)S(1)}, f32[6,768]{1,0:T(8,128)S(1)}, f32[6...) custom-call(bf16[1,1,2,768,768]{4,3,2,1,0:T(8,128)(2,1)S(1)} %copy-d, ...), custom_call_target="tpu_custom_call" | custom-call | tf_op jit(solution)/shard_map/pallas_call | solution.py:480
  82.2 1.3 %shard_map.212 = (bf16[768,768]{1,0:T(8,128)(2,1)}, bf16[768,256]{1,0:T(8,128)(2,1)}, f32[6,768]{1,0:T(8,128)}, f32[6,256]{1,0:T(8,128)}, f32[6,16]{1,0:T(8,128)...) custom-call(bf16[768,768]{1,0:T(8,128)(2,1)S(1)} %get-tuple-element., ...), custom_call_target="tpu_custom_call" | custom-call | tf_op jit(solution)/shard_map/pallas_call | solution.py:514
  83.5 0.2 convert_element_type.10
  83.7 0.7 copy.26
  (4 shorter events, 0.1 us)
Async XLA Ops:
  0.6 1.4 %copy-start.10 = (f32[6,16]{1,0:T(8,128)S(1)}, f32[6,16]{1,0:T(8,128)}, u32[]{:S(2)}) copy-start(f32[6,16]{1,0:T(8,128)} %sch.1) | copy-start | bytes 1156
  0.7 1.4 %copy-start.7 = (f32[6,256]{1,0:T(8,128)S(1)}, f32[6,256]{1,0:T(8,128)}, u32[]{:S(2)}) copy-start(f32[6,256]{1,0:T(8,128)} %sfac.1) | copy-start | bytes 18436
  0.7 1.4 %copy-start.4 = (f32[6,768]{1,0:T(8,128)S(1)}, f32[6,768]{1,0:T(8,128)}, u32[]{:S(2)}) copy-start(f32[6,768]{1,0:T(8,128)} %srec.1) | copy-start | bytes 55300
  0.7 1.4 %copy-start.9 = (f32[6,16]{1,0:T(8,128)S(1)}, f32[6,16]{1,0:T(8,128)}, u32[]{:S(2)}) copy-start(f32[6,16]{1,0:T(8,128)} %fch.1) | copy-start | bytes 1156
  0.7 1.4 %copy-start.6 = (f32[6,256]{1,0:T(8,128)S(1)}, f32[6,256]{1,0:T(8,128)}, u32[]{:S(2)}) copy-start(f32[6,256]{1,0:T(8,128)} %ffac.1) | copy-start | bytes 18436
  0.7 1.4 %copy-start.3 = (f32[6,768]{1,0:T(8,128)S(1)}, f32[6,768]{1,0:T(8,128)}, u32[]{:S(2)}) copy-start(f32[6,768]{1,0:T(8,128)} %frec.1) | copy-start | bytes 55300
  0.7 1.4 %copy-start.8 = (f32[6,16]{1,0:T(8,128)S(1)}, f32[6,16]{1,0:T(8,128)}, u32[]{:S(2)}) copy-start(f32[6,16]{1,0:T(8,128)} %mch.1) | copy-start | bytes 1156
  0.7 1.4 %copy-start.5 = (f32[6,256]{1,0:T(8,128)S(1)}, f32[6,256]{1,0:T(8,128)}, u32[]{:S(2)}) copy-start(f32[6,256]{1,0:T(8,128)} %mfac.1) | copy-start | bytes 18436
  0.7 1.4 %copy-start.2 = (f32[6,768]{1,0:T(8,128)S(1)}, f32[6,768]{1,0:T(8,128)}, u32[]{:S(2)}) copy-start(f32[6,768]{1,0:T(8,128)} %mrec.1) | copy-start | bytes 55300
  0.7 1.4 %copy-start.1 = (bf16[1,1,2,768,256]{4,3,2,1,0:T(8,128)(2,1)S(1)}, bf16[1,1,2,768,256]{4,3,2,1,0:T(8,128)(2,1)}, u32[]{:S(2)}) copy-start(bf16[1,1,2,768,256]{4,3,2,1,0:T(8,128)(2,1)} %fac.1) | copy-start | bytes 2359300
  2.1 1.7 %copy-start = (bf16[1,1,2,768,768]{4,3,2,1,0:T(8,128)(2,1)S(1)}, bf16[1,1,2,768,768]{4,3,2,1,0:T(8,128)(2,1)}, u32[]{:S(2)}) copy-start(bf16[1,1,2,768,768]{4,3,2,1,0:T(8,128)(2,1)} %rec.1) | copy-start | bytes 7077892

commit v4 on v3

--- a/solution.py
+++ b/solution.py
@@ -41,8 +41,8 @@
 def kernel(
     ny, nz, nx,
     rec, fac, chg, mrec, mfac, mch, frec, ffac, fch, srec, sfac, sch,
-    wrec, wfac, wch, omrec, omfac, omch, ofrec, offac, ofch, osrec, osfac, osch,
-    chs, och, own, part, chp, tmp, acc, acz, rbuf, rbuz, zs, zr, ys, yr, xb, sb, sws, swr, n1, n2, hb, ar, bb, zag, asm, w,
+    w, wch, omrec, omfac, omch, ofrec, offac, ofch, osrec, osfac, osch,
+    chs, och, own, part, chp, tmp, acc, acz, rbuf, rbuz, zs, zr, ys, yr, xb, sb, sws, swr, n1, n2, hb, ar, bb, zag, asm,
     own_sem, pair_s, pair_r, chp_s, chp_r, rs_s, rs_r, rz_s, rz_r, z_s, z_r, y_s, y_r, x_s, x_r, sw_sem,
     n1_s, n1_r, n2_s, n2_r, ag_sem, zag_s, zag_r, yag_s, yag_r, pc_s, pc_r, po_s, po_r,
 ):
@@ -414,18 +414,14 @@
                 if s + 1 < steps[st]:
                     yg(st, s + 1).start()
                 pc(st, s).start()
+    for k in range(ny):
+        wch[nz * k : nz * k + nz, :] = w[c, k, 0, cr : cr + 16, :].astype(f32)[0:nz, :]
+
     for h in range(2):
         po(h).wait_recv()
     for st in range(4):
         for s in range(steps[st]):
             pc(st, s).wait_recv()
-    for k in range(ny):
-        r = slice(cr * k, cr * k + cr)
-        wrec[r, 0:256] = w[0, k, 0, 0:cr, :]
-        wrec[r, 256:512] = w[0, k, 1, 0:cr, :]
-        wrec[r, 512:768] = w[1, k, 0, 0:cr, :]
-        wfac[r, :] = w[1, k, 1, 0:cr, :]
-        wch[nz * k : nz * k + nz, :] = w[c, k, 0, cr : cr + 16, :].astype(f32)[0:nz, :]
 
     for i in range(ny):
         pair0(i).wait_send()
@@ -454,12 +450,20 @@
         po(h).wait_send()
 
 
-def write_out(*refs):
-    n = (len(refs) - 1) // 2
-    sem = refs[-1]
-    copies = [
-        pltpu.make_async_copy(refs[i], refs[n + i], sem.at[i]) for i in range(n)
-    ]
+def write_out(ny, cr, w, *refs):
+    n = (len(refs) - 3) // 2
+    wrec, wfac, sem = refs[n], refs[n + 1], refs[-1]
+    pairs = [(refs[i], refs[n + 2 + i]) for i in range(n)]
+    for k in range(ny):
+        r = pl.ds(cr * k, cr)
+        cut = pl.ds(0, cr)
+        pairs += [
+            (w.at[0, k, 0, cut, :], wrec.at[r, pl.ds(0, 256)]),
+            (w.at[0, k, 1, cut, :], wrec.at[r, pl.ds(256, 256)]),
+            (w.at[1, k, 0, cut, :], wrec.at[r, pl.ds(512, 256)]),
+            (w.at[1, k, 1, cut, :], wfac.at[r, :]),
+        ]
+    copies = [pltpu.make_async_copy(p, q, sem.at[i]) for i, (p, q) in enumerate(pairs)]
     for copy in copies:
         copy.start()
     for copy in copies:
@@ -480,11 +484,11 @@
     out = pl.pallas_call(
         functools.partial(kernel, ny, nz, nx),
         out_shape=(
-            sd((rows, 768), bf16), sd((rows, 256), bf16), sd((ny * nz, 256), f32),
+            sd((2, ny, 2, cr + 16, 256), bf16), sd((ny * nz, 256), f32),
         )
         + (sd((6, 768), f32), sd((6, 256), f32), sd((6, 16), f32)) * 3,
         in_specs=[hbm, hbm] + [vm] * 10,
-        out_specs=(vm,) * 12,
+        out_specs=(vm,) * 11,
         scratch_shapes=[
             V((8, 128), f32), V((8, 128), f32),
             V((2, 2, rows, 256), bf16), V((2, 2, rows, 256), bf16), V((ny * nz, 256), f32),
@@ -496,7 +500,6 @@
             V((16, 512), f32), V((8, 512), f32), V((8, 512), f32),
             V((2 * nz, 8, 128), f32), V((ny, 8, 128), f32), V((2, 8, 512), f32), V((8, 512), f32),
             V((16, 512), f32), V((nz, 16, 512), bf16), V((cr + 16, 512), f32),
-            V((2, ny, 2, cr + 16, 256), bf16),
             dma((2,)), dma((2, ny)), dma((2, ny)), dma, dma,
             dma((4, half)), dma((4, half)), dma((4, half)), dma((4, half)),
             dma((nz - 1,)), dma((nz - 1,)), dma((ny - 1,)), dma((ny - 1,)),
@@ -509,16 +512,18 @@
             collective_id=0, has_side_effects=True, vmem_limit_bytes=48_000_000
         ),
     )(rec, fac, chg, mrec, mfac, mch, frec, ffac, fch, srec, sfac, sch)
-    wch = out[2].reshape(ny * nz, 2, 128)[:, :, :96].reshape(rows, 16).astype(bf16)
-    held = out[:2] + out[3:]
+    wch = out[1].reshape(ny * nz, 2, 128)[:, :, :96].reshape(rows, 16).astype(bf16)
+    anywhere = pl.BlockSpec(memory_space=pl.ANY)
+    held = out[2:]
     final = pl.pallas_call(
-        write_out,
-        out_shape=tuple(sd(o.shape, o.dtype) for o in held),
-        in_specs=[pl.BlockSpec(memory_space=pl.ANY)] * len(held),
-        out_specs=(pl.BlockSpec(memory_space=pl.ANY),) * len(held),
-        scratch_shapes=[dma((len(held),))],
+        functools.partial(write_out, ny, cr),
+        out_shape=(sd((rows, 768), bf16), sd((rows, 256), bf16))
+        + tuple(sd(o.shape, o.dtype) for o in held),
+        in_specs=[anywhere] * (1 + len(held)),
+        out_specs=(anywhere,) * (2 + len(held)),
+        scratch_shapes=[dma((4 * ny + len(held),))],
         compiler_params=pltpu.CompilerParams(vmem_limit_bytes=1 << 20),
-    )(*held)
+    )(out[0], *held)
     return (final[0], final[1], wch, *final[2:])
 
 

time: 84.6 us -> 92.5 us (1.093)
  local copies, waits for them, and re-layouts: 2.98 us -> 10.4 us
    unnamed x24, local copies, waits for them, and re-layouts: 2.44 us -> 9.89 us
where the time goes in v4:
time: 92.5 us; the launch traced here: 91.8 us
  Pallas kernels  79.8 us (86%)
  local copies, waits for them, and re-layouts  10.4 us (11%)
    pallas_call x1, Pallas kernels, body(): pl.pallas_call(functools.partial(kernel, ny, nz, nx), out_shape=(sd((2, n...  78.3 us
    unnamed x24, local copies, waits for them, and re-layouts  9.89 us

profile of v4, /device:TPU:1, one launch (start us, length us, event | category | flops | bytes accessed | tf_op | source)
XLA Modules:
  0.0 91.8 jit_solution(5115964282361784635)
XLA Ops:
  0.6 0.8 convert_reduce_fusion
  1.5 0.2 copy.25
  1.6 0.2 reshape.36
  1.9 0.0 copy-start
  1.9 1.7 %copy-done = bf16[1,1,2,768,768]{4,3,2,1,0:T(8,128)(2,1)S(1)} copy-done((bf16[1,1,2,768,768]{4,3,2,1,0:T(8,128)(2,1)S(1)}, bf16[1,1,2,768,768]{4,3,2,1,0:T(8,128)(2,1)}, u32[]{:S(2)}) %copy-start) | copy-done | bytes 2359320
  3.5 0.0 copy-start.1
  3.5 1.1 %copy-done.1 = bf16[1,1,2,768,256]{4,3,2,1,0:T(8,128)(2,1)S(1)} copy-done((bf16[1,1,2,768,256]{4,3,2,1,0:T(8,128)(2,1)S(1)}, bf16[1,1,2,768,256]{4,3,2,1,0:T(8,128)(2,1)}, u32[]{:S(2)}) %copy-start.1) | copy-done | bytes 786456
  4.7 0.0 copy-start.2
  4.7 0.7 copy-done.2
  5.4 0.0 copy-start.3
  5.4 0.7 copy-done.3
  6.1 0.0 copy-start.4
  6.1 0.7 copy-done.4
  6.9 0.0 copy-start.5
  6.9 0.7 copy-done.5
  7.6 0.0 copy-start.6
  7.6 0.7 copy-done.6
  8.3 0.0 copy-start.7
  8.3 0.7 copy-done.7
  9.0 0.0 copy-start.8
  9.0 0.7 copy-done.8
  9.7 0.0 copy-start.9
  9.7 0.7 copy-done.9
  10.3 0.0 copy-start.10
  10.3 0.7 copy-done.10
  11.0 78.3 %shard_map.211 = (bf16[2,8,2,112,256]{4,3,2,1,0:T(8,128)(2,1)S(1)}, f32[64,256]{1,0:T(8,128)S(1)}, f32[6,768]{1,0:T(8,128)S(1)}, f32[6,256]{1,0:T(8,128)S(1)}, f...) custom-call(bf16[1,1,2,768,768]{4,3,2,1,0:T(8,128)(2,1)S(1)} %copy-d, ...), custom_call_target="tpu_custom_call" | custom-call | tf_op jit(solution)/shard_map/pallas_call | solution.py:484
  89.3 1.5 %shard_map.212 = (bf16[768,768]{1,0:T(8,128)(2,1)}, bf16[768,256]{1,0:T(8,128)(2,1)}, f32[6,768]{1,0:T(8,128)}, f32[6,256]{1,0:T(8,128)}, f32[6,16]{1,0:T(8,128)...) custom-call(bf16[2,8,2,112,256]{4,3,2,1,0:T(8,128)(2,1)S(1)} %get-tu, ...), custom_call_target="tpu_custom_call" | custom-call | tf_op jit(solution)/shard_map/pallas_call | solution.py:518
  90.9 0.2 convert_element_type.10
  91.1 0.7 copy.26
  (4 shorter events, 0.1 us)
Async XLA Ops:
  1.9 1.7 %copy-start = (bf16[1,1,2,768,768]{4,3,2,1,0:T(8,128)(2,1)S(1)}, bf16[1,1,2,768,768]{4,3,2,1,0:T(8,128)(2,1)}, u32[]{:S(2)}) copy-start(bf16[1,1,2,768,768]{4,3,2,1,0:T(8,128)(2,1)} %rec.1) | copy-start | bytes 7077892
  3.5 1.1 %copy-start.1 = (bf16[1,1,2,768,256]{4,3,2,1,0:T(8,128)(2,1)S(1)}, bf16[1,1,2,768,256]{4,3,2,1,0:T(8,128)(2,1)}, u32[]{:S(2)}) copy-start(bf16[1,1,2,768,256]{4,3,2,1,0:T(8,128)(2,1)} %fac.1) | copy-start | bytes 2359300
  4.7 0.7 copy-start.2
  5.4 0.7 copy-start.3
  6.1 0.7 copy-start.4
  6.9 0.7 copy-start.5
  7.6 0.7 copy-start.6
  8.3 0.7 copy-start.7
  9.0 0.7 copy-start.8
  9.7 0.7 copy-start.9
  10.3 0.7 copy-start.10
